TPU v7x, 256 devices: a whole 4x4x8 slice. The times are simulated.
256 devices in a mesh: orient: 16 (over x, y_hi, core), pix: 16 (over y_lo, z).
Axes of the slice: x: 4, y: 4 (y_hi: 2, y_lo: 2; y = y_hi * 2 + y_lo), z: 8, core: 2. Of those that a mesh axis runs over, the one named last changes fastest.
Arguments:
- model: bfloat16 [12288, 65536], P('orient', 'pix'), may hold values from 0.012 to 3.32
- patterns: int32 [384, 65536], P(None, 'pix'), may hold values from 0 to 10, as said below
Outputs:
- updated: bfloat16 [12288, 65536], P('orient', 'pix')
Inputs may be any that keep to these rules, and one draw needn't show every extreme that they name: `patterns`: each pattern has a brightness level of its own; its counts are whole numbers from 0 to one less than that level.
All inputs are finite; a program needn't handle non-finite values.
Results may differ from a plain program's by a relative error of at most 0.0022.
Values may be sent and summed in bfloat16 or wider, within the bound.
A program may use at most 64 MiB of HBM per device.

v0:
```python
import math

import jax
import jax.numpy as jnp
from jax import lax
from jax.sharding import PartitionSpec as P

PIX = 65536


prior_weight = 1.0


def normalize(scores):
    highest = jnp.max(scores, axis=0)
    overall = lax.pmax(highest, "orient")
    scaled = jnp.exp(scores - overall[None, :])
    exp_total = lax.psum(jnp.sum(scaled, axis=0), "orient")
    return (scaled / exp_total[None, :]).astype(jnp.bfloat16)


def on_device(model, patterns):
    anneal_beta = 2.0 / math.sqrt(PIX)
    counts = patterns.astype(jnp.float32)
    state = model
    intensity = state.astype(jnp.float32)
    log_slices = jnp.log(intensity)
    products = lax.dot_general(
        log_slices,
        counts,
        (((1,), (1,)), ((), ())),
        precision=lax.Precision.HIGHEST,
        preferred_element_type=jnp.float32,
    )
    local_totals = jnp.sum(intensity, axis=1)
    totals = lax.psum(local_totals, "pix")
    summed = lax.psum(products, "pix")
    likelihood = summed - totals[:, None]
    probs = normalize(anneal_beta * likelihood)
    wide_probs = probs.astype(jnp.float32)
    numerator = jnp.dot(
        wide_probs, counts, precision=lax.Precision.HIGHEST, preferred_element_type=jnp.float32
    )
    normalizer = jnp.sum(wide_probs, axis=1)
    state = ((numerator + prior_weight * intensity) / (normalizer[:, None] + prior_weight)).astype(
        jnp.bfloat16
    )
    return state


def solution(mesh):
    placed = (P("orient", "pix"), P(None, "pix"))
    return jax.shard_map(
        on_device, mesh=mesh, in_specs=placed, out_specs=P("orient", "pix"), check_vma=False
    )
```

profile of v0, /device:TPU:1, one launch (start us, length us, event | category | flops | bytes accessed | tf_op | source)
XLA Modules:
  0.0 267.3 jit_solution(10100605636570252228)
XLA Ops:
  6.5 0.0 all-reduce.2.cloned.1.call-start
  6.5 24.2 %fusion = f32[768,384]{1,0:T(8,128)} fusion(bf16[768,4096]{1,0:T(8,128)(2,1)} %param.2, s32[384,4096]{1,0:T(8,128)} %param.3), kind=kOutput, calls=%fused_computation.3 | convolution fusion | flops 14500233216 | bytes 13762560 | tf_op jit(solution)/shard_map/dot_general | solution.py:28
  30.8 0.0 all-reduce.2.cloned.1.call-update
  30.8 3.7 %convert_reduce_fusion = f32[768]{0:T(1024)S(1)} fusion(bf16[768,4096]{1,0:T(8,128)(2,1)} %param.2), kind=kLoop, calls=%fused_computation.1 | loop fusion | flops 6290688 | bytes 6294528 | tf_op jit(solution)/shard_map/reduce_sum | solution.py:35
  34.5 31.9 %psum.22 = f32[768]{0:T(1024)S(1)} all-reduce(f32[768]{0:T(1024)S(1)} %convert_reduce_fusion), channel_id=1, replica_groups=mesh['orient'=16,'pix'=16] {'pix'}, use_global_device_ids=true, to_apply=%region_2.0 | all-reduce | flops 768 | bytes 6144 | tf_op jit(solution)/shard_map/psum | solution.py:36
  66.4 96.0 %all-reduce.2.cloned.1.call-done = f32[768,384]{1,0:T(8,128)} async-done(((f32[768,384]{1,0:T(8,128)}), f32[768,384]{1,0:T(8,128)}) %all-reduce.2.cloned.1.call-update) | async-done | bytes 1179664 | tf_op jit(solution)/shard_map/psum | solution.py:37
  162.4 0.0 copy-start
  162.4 1.6 fusion.5
  164.0 44.2 %pmax.7 = f32[384]{0:T(512)S(1)} all-reduce(f32[384]{0:T(512)S(1)} %fusion.5), channel_id=1, replica_groups=mesh['orient'=16,'pix'=16] {'orient'}, use_global_device_ids=true, to_apply=%region_4.0 | all-reduce | flops 384 | bytes 3072 | tf_op jit(solution)/shard_map/pmax | solution.py:16
  208.1 0.0 copy-done
  208.1 0.3 fusion.6
  208.5 33.2 %psum.23 = f32[384]{0:T(512)S(1)} all-reduce(f32[384]{0:T(512)S(1)} %fusion.6), channel_id=1, replica_groups=mesh['orient'=16,'pix'=16] {'orient'}, use_global_device_ids=true, to_apply=%region_6.0 | all-reduce | flops 384 | bytes 3072 | tf_op jit(solution)/shard_map/psum | solution.py:18
  241.6 0.5 convert_reduce_fusion.1
  242.1 18.3 %fusion.2 = bf16[768,4096]{1,0:T(8,128)(2,1)} fusion(bf16[768,4096]{1,0:T(8,128)(2,1)} %param.2, bf16[768,384]{1,0:T(8,128)(2,1)S(1)} %get-tuple-element.6, f32[768]{0:T(1024)S(1)} %broadcast_add_fusion, s32[384,4096]{1,0:T(8,128)} %param.3), kind=kOutput, calls=%fused_computation.5 | convolution fusion | flops 14509670400 | bytes 19467264 | tf_op jit(solution)/shard_map/dot_general | solution.py:41
  (1 shorter events, 0.0 us)
Async XLA Ops:
  6.5 155.9 %all-reduce.2.cloned.1.call-start = ((), (), s32[]{:S(2)}) async-start(), calls=%async_computation | async-start | bytes 2359296 | tf_op jit(solution)/shard_map/psum | solution.py:37
  162.4 45.8 %copy-start = (f32[768,384]{1,0:T(8,128)S(1)}, f32[768,384]{1,0:T(8,128)}, u32[]{:S(2)}) copy-start(f32[768,384]{1,0:T(8,128)} %all-reduce.2.cloned.1.call-done) | copy-start | bytes 3538948
Sparse Core Ops, SparseCore 0:
  30.9 131.4 all-reduce.1
where the time goes:
time: 267 us
  blocking collectives  109 us (41%)
  waiting for transfers between devices  96 us (36%)
  matrix products  42.5 us (16%)
  between operations  13.4 us (5%)
  other arithmetic  6.02 us (2%)
    psum x1, waiting for transfers between devices, on_device(): summed = lax.psum(products, 'pix')  96 us
    pmax x1, blocking collectives, normalize(): overall = lax.pmax(highest, 'orient')  44.2 us
    psum x1, blocking collectives, normalize(): exp_total = lax.psum(jnp.sum(scaled, axis=0), 'orient')  33.2 us
    psum x1, blocking collectives, on_device(): totals = lax.psum(local_totals, 'pix')  31.9 us
    dot_general x1, matrix products, on_device(): lax.dot_general(log_slices, counts, (((1,), (1,)), ((), ())), precision=l...  24.2 us
    dot_general x1, matrix products, on_device(): jnp.dot(wide_probs, counts, precision=lax.Precision.HIGHEST, preferred_el...  18.3 us
  transfers between devices with their start and end apart: 1, of which 1 were waited for; matrix products, arithmetic and copies ran while one was open for 1% of the time, Pallas kernels for 0%

commit v1 on v0

v1 whole, which is shorter than its diff:
```python
import functools
import math

import jax
import jax.numpy as jnp
from jax import lax
from jax.experimental import pallas as pl
from jax.experimental.pallas import tpu as pltpu
from jax.sharding import PartitionSpec as P

PIX = 65536
BETA = 2.0 / math.sqrt(PIX)
MESH = pl.DeviceIdType.MESH

ROWS = 768
COLS = 4096
FRAMES = 384
KC = 512
NK = COLS // KC
NB = 3
BS = ROWS // NB
HALF = BS // 2
NZ = 8
OWN = FRAMES // NZ
NORIENT = 16


def exchange_kernel(
    model_ref,
    pat_ref,
    probs_ref,
    counts_out,
    mv,
    pv,
    cb,
    part,
    tot,
    recv,
    score,
    own_e,
    all_e,
    stat_own,
    stat_all,
    fac_own,
    fac_all,
    pat_sem,
    mod_sem,
    cnt_sem,
    rs_send,
    rs_recv,
    ag_send,
    ag_recv,
    st_send,
    st_recv,
    fc_send,
    fc_recv,
):
    o = lax.axis_index("orient")
    p = lax.axis_index("pix")
    y = p // NZ
    z = lax.rem(p, NZ)

    def pix_peer(dy, dz):
        py = lax.rem(y + dy, 2)
        pz = lax.rem(z + dz, NZ)
        return py, pz

    pix_offsets = [(dy, dz) for dz in (4, 3, 5, 2, 6, 1, 7, 0) for dy in (1, 0) if (dy, dz) != (0, 0)]
    plane_offsets = [(dy, do) for do in range(NORIENT) for dy in (1, 0) if (dy, do) != (0, 0)]

    def pat_copy(k):
        return pltpu.make_async_copy(
            pat_ref.at[:, pl.ds(k * KC, KC)], pv.at[k], pat_sem.at[k]
        )

    def mod_copy(b, k):
        return pltpu.make_async_copy(
            model_ref.at[pl.ds(b * BS, BS), pl.ds(k * KC, KC)],
            mv.at[b, k],
            mod_sem.at[b, k],
        )

    for k in range(NK):
        pat_copy(k).start()
        mod_copy(0, k).start()
    for b in range(1, NB):
        for k in range(NK):
            mod_copy(b, k).start()

    barrier = pltpu.get_barrier_semaphore()
    for dy, dz in pix_offsets:
        py, pz = pix_peer(dy, dz)
        pl.semaphore_signal(barrier, inc=1, device_id=(o, py * NZ + pz), device_id_type=MESH)
    for dy, do in plane_offsets:
        if do == 0:
            continue
        py, _ = pix_peer(dy, 0)
        pl.semaphore_signal(
            barrier, inc=1, device_id=(lax.rem(o + do, NORIENT), py * NZ + z), device_id_type=MESH
        )

    def rs_copy(b, dy, dz):
        py, pz = pix_peer(dy, dz)
        slot = dy * NZ + (NZ - dz) % NZ - 1
        return pltpu.make_async_remote_copy(
            src_ref=part.at[2 * b + py, pl.ds(pl.multiple_of(pz * OWN, 8), OWN), :],
            dst_ref=recv.at[b, slot],
            send_sem=rs_send,
            recv_sem=rs_recv.at[b],
            device_id=(o, py * NZ + pz),
            device_id_type=MESH,
        )

    ones = jnp.ones((8, 128), jnp.float32)

    for b in range(NB):
        part[2 * b] = jnp.zeros((FRAMES, HALF), jnp.float32)
        part[2 * b + 1] = jnp.zeros((FRAMES, HALF), jnp.float32)
        tot[...] = jnp.zeros_like(tot)

        def chunk(k, carry, b=b):
            mod_copy(b, k).wait()
            if b == 0:
                pat_copy(k).wait()
                cb[k] = pv[k].astype(jnp.float32).astype(jnp.bfloat16)
            x = mv[b, k].astype(jnp.float32)
            t = tot[...]
            for j in range(KC // 128):
                t = t + x[:, j * 128 : (j + 1) * 128]
            tot[...] = t
            logs = jnp.log(x)
            hi = logs.astype(jnp.bfloat16)
            lo = (logs - hi.astype(jnp.float32)).astype(jnp.bfloat16)
            c = cb[k]
            d = lax.dot_general(
                jnp.concatenate([c, c], axis=1),
                jnp.concatenate([hi, lo], axis=1),
                (((1,), (1,)), ((), ())),
                preferred_element_type=jnp.float32,
            )
            part[2 * b] += d[:, :HALF]
            part[2 * b + 1] += d[:, HALF:]
            return carry

        lax.fori_loop(0, NK, chunk, 0)
        row = lax.dot_general(
            ones,
            tot[...],
            (((1,), (1,)), ((), ())),
            precision=lax.Precision.HIGHEST,
            preferred_element_type=jnp.float32,
        )
        part[2 * b] -= row[0:1, :HALF]
        part[2 * b + 1] -= row[0:1, HALF:]
        if b == 0:
            pltpu.make_async_copy(cb, counts_out, cnt_sem).start()
            pl.semaphore_wait(barrier, len(pix_offsets) + len(plane_offsets) - 1)
        for dy, dz in pix_offsets:
            rs_copy(b, dy, dz).start()

    npix = len(pix_offsets)
    for b in range(NB):
        pltpu.make_async_copy(recv.at[b], recv.at[b], rs_recv.at[b]).wait()
        total = part[2 * b + y, pl.ds(pl.multiple_of(z * OWN, 8), OWN), :]
        for j in range(npix):
            total = total + recv[b, j]
        score[b] = BETA * total

    s = [score[b] for b in range(NB)]
    top = jnp.maximum(jnp.maximum(s[0], s[1]), s[2])
    m = jnp.max(top, axis=1, keepdims=True)
    acc = jnp.zeros((OWN, HALF), jnp.float32)
    for b in range(NB):
        e = jnp.exp(s[b] - m)
        acc = acc + e
        own_e[b] = e.astype(jnp.bfloat16)
    esum = jnp.sum(acc, axis=1, keepdims=True)
    eye = lax.broadcasted_iota(jnp.int32, (OWN, 128), 0) == lax.broadcasted_iota(
        jnp.int32, (OWN, 128), 1
    )
    m_row = jnp.sum(jnp.where(eye, m, 0.0), axis=0, keepdims=True)
    s_row = jnp.sum(jnp.where(eye, esum, 0.0), axis=0, keepdims=True)
    upper = lax.broadcasted_iota(jnp.int32, (8, 128), 0) < 4
    stat_own[...] = jnp.where(upper, m_row, s_row)

    def stat_copy(j, dy, do):
        py, _ = pix_peer(dy, 0)
        slot = dy * NORIENT + (NORIENT - do) % NORIENT - 1
        return pltpu.make_async_remote_copy(
            src_ref=stat_own,
            dst_ref=stat_all.at[slot],
            send_sem=st_send,
            recv_sem=st_recv,
            device_id=(lax.rem(o + do, NORIENT), py * NZ + z),
            device_id_type=MESH,
        )

    for j, (dy, do) in enumerate(plane_offsets):
        stat_copy(j, dy, do).start()

    def ag_copy(dy, dz):
        py, pz = pix_peer(dy, dz)
        return pltpu.make_async_remote_copy(
            src_ref=own_e,
            dst_ref=all_e.at[y * NZ + z],
            send_sem=ag_send,
            recv_sem=ag_recv,
            device_id=(o, py * NZ + pz),
            device_id_type=MESH,
        )

    for dy, dz in pix_offsets:
        ag_copy(dy, dz).start()

    nplane = len(plane_offsets)
    pltpu.make_async_copy(stat_all, stat_all, st_recv).wait()
    big = m_row
    for j in range(nplane):
        big = jnp.maximum(big, stat_all[j, 0:1, :])
    whole = s_row * jnp.exp(m_row - big)
    for j in range(nplane):
        whole = whole + stat_all[j, 4:5, :] * jnp.exp(stat_all[j, 0:1, :] - big)
    lane = lax.broadcasted_iota(jnp.int32, (1, 128), 1)
    whole = jnp.where(lane < OWN, whole, 1.0)
    factor = jnp.exp(m_row - big) / whole
    fac_own[...] = jnp.broadcast_to(factor, (8, 128))

    def fac_copy(dy, dz):
        py, pz = pix_peer(dy, dz)
        return pltpu.make_async_remote_copy(
            src_ref=fac_own,
            dst_ref=fac_all.at[y * NZ + z],
            send_sem=fc_send,
            recv_sem=fc_recv,
            device_id=(o, py * NZ + pz),
            device_id_type=MESH,
        )

    for dy, dz in pix_offsets:
        fac_copy(dy, dz).start()
    fac_all[y * NZ + z] = fac_own[...]
    all_e[y * NZ + z] = own_e[...]

    fac_sent = fac_all.at[pl.ds(0, npix)]
    e_sent = all_e.at[pl.ds(0, npix)]
    pltpu.make_async_copy(fac_sent, fac_sent, fc_recv).wait()
    pltpu.make_async_copy(e_sent, e_sent, ag_recv).wait()

    for yy in range(2):
        cols = []
        for zz in range(NZ):
            f = jnp.sum(jnp.where(eye, fac_all[yy * NZ + zz, 0:1, :], 0.0), axis=1, keepdims=True)
            cols.append(f)
        for b in range(NB):
            block = jnp.concatenate(
                [all_e[yy * NZ + zz, b].astype(jnp.float32) * cols[zz] for zz in range(NZ)], axis=0
            )
            r = (2 * b + yy) * HALF
            probs_ref[r : r + HALF, :] = block.T.astype(jnp.bfloat16)

    pltpu.make_async_copy(cb, counts_out, cnt_sem).wait()
    pltpu.make_async_copy(recv, recv, rs_send).wait()
    pltpu.make_async_copy(e_sent, e_sent, ag_send).wait()
    pltpu.make_async_copy(stat_all, stat_all, st_send).wait()
    pltpu.make_async_copy(fac_sent, fac_sent, fc_send).wait()


def update_kernel(probs_ref, counts_ref, model_ref, out_ref, inv):
    @pl.when(pl.program_id(0) == 0)
    def _():
        norm = jnp.sum(probs_ref[...].astype(jnp.float32), axis=1, keepdims=True)
        inv[...] = jnp.broadcast_to(1.0 / (norm + 1.0), inv.shape)

    num = jnp.dot(probs_ref[...], counts_ref[0], preferred_element_type=jnp.float32)
    x = model_ref[...].astype(jnp.float32)
    scale = jnp.concatenate([inv[...]] * (KC // 128), axis=1)
    out_ref[...] = ((num + x) * scale).astype(jnp.bfloat16)


def on_device(model, patterns):
    f32, bf16 = jnp.float32, jnp.bfloat16
    dma = pltpu.SemaphoreType.DMA
    probs, counts = pl.pallas_call(
        exchange_kernel,
        name="exchange",
        out_shape=(
            jax.ShapeDtypeStruct((ROWS, FRAMES), bf16),
            jax.ShapeDtypeStruct((NK, FRAMES, KC), bf16),
        ),
        in_specs=[pl.BlockSpec(memory_space=pl.ANY)] * 2,
        out_specs=(
            pl.BlockSpec(memory_space=pltpu.VMEM),
            pl.BlockSpec(memory_space=pl.ANY),
        ),
        scratch_shapes=[
            pltpu.VMEM((NB, NK, BS, KC), bf16),
            pltpu.VMEM((NK, FRAMES, KC), jnp.int32),
            pltpu.VMEM((NK, FRAMES, KC), bf16),
            pltpu.VMEM((2 * NB, FRAMES, HALF), f32),
            pltpu.VMEM((BS, 128), f32),
            pltpu.VMEM((NB, 15, OWN, HALF), f32),
            pltpu.VMEM((NB, OWN, HALF), f32),
            pltpu.VMEM((NB, OWN, HALF), bf16),
            pltpu.VMEM((2 * NZ, NB, OWN, HALF), bf16),
            pltpu.VMEM((8, 128), f32),
            pltpu.VMEM((31, 8, 128), f32),
            pltpu.VMEM((8, 128), f32),
            pltpu.VMEM((2 * NZ, 8, 128), f32),
            dma((NK,)),
            dma((NB, NK)),
            dma,
            dma,
            dma((NB,)),
            dma,
            dma,
            dma,
            dma,
            dma,
            dma,
        ],
        compiler_params=pltpu.CompilerParams(
            collective_id=0, has_side_effects=True, vmem_limit_bytes=40 * 1024 * 1024
        ),
    )(model, patterns)
    return pl.pallas_call(
        update_kernel,
        name="update",
        grid=(NK,),
        out_shape=jax.ShapeDtypeStruct((ROWS, COLS), bf16),
        in_specs=[
            pl.BlockSpec((ROWS, FRAMES), lambda i: (0, 0)),
            pl.BlockSpec((1, FRAMES, KC), lambda i: (i, 0, 0)),
            pl.BlockSpec((ROWS, KC), lambda i: (0, i)),
        ],
        out_specs=pl.BlockSpec((ROWS, KC), lambda i: (0, i)),
        scratch_shapes=[pltpu.VMEM((ROWS, 128), f32)],
        compiler_params=pltpu.CompilerParams(vmem_limit_bytes=20 * 1024 * 1024),
    )(probs, counts, model)


def solution(mesh):
    placed = (P("orient", "pix"), P(None, "pix"))
    return jax.shard_map(
        on_device, mesh=mesh, in_specs=placed, out_specs=P("orient", "pix"), check_vma=False
    )
```

time: 267 us -> 66.1 us (0.25)
  the two profiles are of different devices: /device:TPU:1 before, /device:TPU:6 now
where the time goes in v1:
time: 66.1 us; the launch traced here: 65 us
  Pallas kernels  62.2 us (94%)
  local copies, waits for them, and re-layouts  2.78 us (4%)
    pallas_call x1, Pallas kernels, on_device(): pl.pallas_call(exchange_kernel, name='exchange', out_shape=(jax.ShapeDtyp...  55.3 us
    pallas_call x1, Pallas kernels, on_device(): pl.pallas_call(update_kernel, name='update', grid=(NK,), out_shape=jax.Sh...  6.91 us
    unnamed x2, local copies, waits for them, and re-layouts  2.78 us

profile of v1, /device:TPU:6, one launch (start us, length us, event | category | flops | bytes accessed | tf_op | source)
XLA Modules:
  0.0 65.0 jit_solution(11676203601834891996)
XLA Ops:
  0.0 0.0 copy-start
  0.0 2.8 %copy-done = bf16[768,4096]{1,0:T(8,128)(2,1)S(1)} copy-done((bf16[768,4096]{1,0:T(8,128)(2,1)S(1)}, bf16[768,4096]{1,0:T(8,128)(2,1)}, u32[]{:S(2)}) %copy-start) | copy-done | bytes 6291480
  2.8 55.3 %exchange.1 = (bf16[768,384]{1,0:T(8,128)(2,1)S(1)}, bf16[8,384,512]{2,1,0:T(8,128)(2,1)S(1)}) custom-call(bf16[768,4096]{1,0:T(8,128)(2,1)S(1)} %copy-done, s32[384,4096]{1,0:T(8,128)} %pat_ref.1), custom_call_target="tpu_custom_call" | custom-call | tf_op jit(solution)/shard_map/exchange/pallas_call | solution.py:283
  58.1 6.9 %update.1 = bf16[768,4096]{1,0:T(8,128)(2,1)} custom-call(bf16[768,384]{1,0:T(8,128)(2,1)S(1)} %get-tuple-element.7.probs_ref, bf16[8,384,512]{2,1,0:T(8,128)(2,1)S(1)} %get-tuple-element.8.counts_ref, bf16[768,4096]{1,0:T(8,128)(2,1)S(1)} %copy-done), custom_call_target="tpu_custom_call" | custom-call | tf_op jit(solution)/shard_map/update/pallas_call | solution.py:325
Async XLA Ops:
  0.0 2.8 %copy-start = (bf16[768,4096]{1,0:T(8,128)(2,1)S(1)}, bf16[768,4096]{1,0:T(8,128)(2,1)}, u32[]{:S(2)}) copy-start(bf16[768,4096]{1,0:T(8,128)(2,1)} %model_ref.3) | copy-start | bytes 18874372

commit v2 on v1

v2 whole, which is shorter than its diff:
```python
import math

import jax
import jax.numpy as jnp
from jax import lax
from jax.experimental import pallas as pl
from jax.experimental.pallas import tpu as pltpu
from jax.sharding import PartitionSpec as P

PIX = 65536
BETA = 2.0 / math.sqrt(PIX)
MESH = pl.DeviceIdType.MESH

ROWS = 768
COLS = 4096
FRAMES = 384
KC = 512
NK = COLS // KC
NB = 3
BS = ROWS // NB
NZ = 8
OWN = FRAMES // NZ
NORIENT = 16
UNROLL = 4

RS_HOPS = ((4, 3), (3, 4), (4, 3))
AG_HOPS = ((4, 3), (3, 4), (4, 3))


def exchange_kernel(
    model_ref,
    pat_ref,
    probs_ref,
    cb,
    mv,
    pv,
    part,
    tot,
    recv,
    y_out,
    y_in,
    all_e,
    stat_own,
    stat_all,
    fac_own,
    fac_all,
    pat_sem,
    mod_sem,
    rs_send,
    rs_recv,
    y_send,
    y_recv,
    ag_send,
    ag_recv,
    st_send,
    st_recv,
    fc_send,
    fc_recv,
):
    o = lax.axis_index("orient")
    p = lax.axis_index("pix")
    y = p // NZ
    z = lax.rem(p, NZ)

    def at_z(dz):
        return (o, y * NZ + lax.rem(z + dz + NZ, NZ))

    y_peer = (o, (1 - y) * NZ + z)
    orient_peers = [(do, (lax.rem(o + do, NORIENT), p)) for do in range(1, NORIENT)]

    def pat_copy(k):
        return pltpu.make_async_copy(
            pat_ref.at[:, pl.ds(k * KC, KC)], pv.at[k], pat_sem.at[k]
        )

    def mod_copy(b, k):
        return pltpu.make_async_copy(
            model_ref.at[pl.ds(b * BS, BS), pl.ds(k * KC, KC)],
            mv.at[b, k],
            mod_sem.at[b, k],
        )

    for k in range(NK):
        pat_copy(k).start()
        mod_copy(0, k).start()
    for b in range(1, NB):
        for k in range(NK):
            mod_copy(b, k).start()

    barrier = pltpu.get_barrier_semaphore()
    for dz in range(1, NZ):
        pl.semaphore_signal(barrier, inc=1, device_id=at_z(dz), device_id_type=MESH)
    pl.semaphore_signal(barrier, inc=1, device_id=y_peer, device_id_type=MESH)
    for _, peer in orient_peers:
        pl.semaphore_signal(barrier, inc=1, device_id=peer, device_id_type=MESH)

    def own_part(b, c):
        row = pl.multiple_of(lax.rem(c + NZ, NZ) * OWN, 8)
        return part.at[b, pl.ds(row, OWN), :]

    def rs_slot(b, way, step):
        return sum(sum(h) for h in RS_HOPS[:b]) + (RS_HOPS[b][0] if way else 0) + step - 1

    def rs_copy(b, way, step):
        hops = RS_HOPS[b][way]
        sign = 1 if way else -1
        slot = rs_slot(b, way, step)
        left = hops - step + 1
        src = own_part(b, z + sign * left) if step == 1 else recv.at[slot - 1]
        return pltpu.make_async_remote_copy(
            src_ref=src,
            dst_ref=recv.at[slot],
            send_sem=rs_send,
            recv_sem=rs_recv.at[slot],
            device_id=at_z(sign),
            device_id_type=MESH,
        )

    def rs_start(b):
        for way in range(2):
            rs_copy(b, way, 1).start()

    def rs_step(b, step):
        for way in range(2):
            hops = RS_HOPS[b][way]
            if step > hops:
                continue
            rs_copy(b, way, step).wait_recv()
            if step < hops:
                sign = 1 if way else -1
                slot = rs_slot(b, way, step)
                recv[slot] += own_part(b, z + sign * (hops - step))[...]
                rs_copy(b, way, step + 1).start()

    def y_copy(b):
        return pltpu.make_async_remote_copy(
            src_ref=y_out.at[b],
            dst_ref=y_in.at[b],
            send_sem=y_send,
            recv_sem=y_recv.at[b],
            device_id=y_peer,
            device_id_type=MESH,
        )

    def rs_end(b):
        low = recv[rs_slot(b, 0, RS_HOPS[b][0])]
        high = recv[rs_slot(b, 1, RS_HOPS[b][1])]
        y_out[b] = own_part(b, z)[...] + (low + high)
        y_copy(b).start()

    ones = jnp.ones((8, 128), jnp.float32)

    def chunk(b, k):
        if b == 0:
            mod_copy(b, k).wait()
            pat_copy(k).wait()
            cb[k] = pv[k].astype(jnp.float32).astype(jnp.bfloat16)
        x = mv[b, k].astype(jnp.float32)
        t = tot[b]
        for j in range(KC // 128):
            t = t + x[:, j * 128 : (j + 1) * 128]
        tot[b] = t
        logs = jnp.log(x)
        hi = logs.astype(jnp.bfloat16)
        lo = (logs - hi.astype(jnp.float32)).astype(jnp.bfloat16)
        c = cb[k]
        part[b] += lax.dot_general(
            jnp.concatenate([c, c], axis=1),
            jnp.concatenate([hi, lo], axis=1),
            (((1,), (1,)), ((), ())),
            preferred_element_type=jnp.float32,
        )

    def finish(b):
        row = lax.dot_general(
            ones,
            tot[b],
            (((1,), (1,)), ((), ())),
            precision=lax.Precision.HIGHEST,
            preferred_element_type=jnp.float32,
        )
        part[b] -= row[0:1, :]

    hooks = {(1, 4): [("step", 0, 1)], (2, 4): [("step", 0, 2), ("step", 1, 1)]}
    tail = [
        ("step", 2, 1),
        ("step", 1, 2),
        ("step", 0, 3),
        ("step", 2, 2),
        ("step", 1, 3),
        ("step", 0, 4),
        ("end", 0),
        ("step", 2, 3),
        ("step", 1, 4),
        ("end", 1),
        ("step", 2, 4),
        ("end", 2),
    ]

    def act(hook):
        kind, b = hook[0], hook[1]
        if kind == "start":
            if b == 0:
                pl.semaphore_wait(barrier, NZ + len(orient_peers))
            rs_start(b)
        elif kind == "step":
            rs_step(b, hook[2])
        else:
            rs_end(b)

    tot[...] = jnp.zeros_like(tot)
    for b in range(NB):
        part[b] = jnp.zeros((FRAMES, BS), jnp.float32)
        if b == 0:
            lax.fori_loop(0, NK, lambda k, carry: (chunk(0, k), carry)[1], 0)
        else:
            for k in range(NK):
                mod_copy(b, k).wait()
            for first in range(0, NK, UNROLL):
                for k in range(first, first + UNROLL):
                    chunk(b, k)
                for hook in hooks.get((b, first), ()):
                    act(hook)
        finish(b)
        act(("start", b))
    for hook in tail:
        act(hook)

    scores = []
    for b in range(NB):
        y_copy(b).wait_recv()
        scores.append(BETA * (y_out[b] + y_in[b]))

    m = jnp.max(jnp.maximum(jnp.maximum(scores[0], scores[1]), scores[2]), axis=1, keepdims=True)
    acc = jnp.zeros((OWN, BS), jnp.float32)
    for b in range(NB):
        e = jnp.exp(scores[b] - m)
        acc = acc + e
        all_e[z, b] = e.astype(jnp.bfloat16)
    esum = jnp.sum(acc, axis=1, keepdims=True)
    eye = lax.broadcasted_iota(jnp.int32, (OWN, 128), 0) == lax.broadcasted_iota(
        jnp.int32, (OWN, 128), 1
    )
    m_row = jnp.sum(jnp.where(eye, m, 0.0), axis=0, keepdims=True)
    s_row = jnp.sum(jnp.where(eye, esum, 0.0), axis=0, keepdims=True)
    upper = lax.broadcasted_iota(jnp.int32, (8, 128), 0) < 4
    stat_own[...] = jnp.where(upper, m_row, s_row)

    def stat_copy(do, peer):
        return pltpu.make_async_remote_copy(
            src_ref=stat_own,
            dst_ref=stat_all.at[NORIENT - do - 1],
            send_sem=st_send,
            recv_sem=st_recv,
            device_id=peer,
            device_id_type=MESH,
        )

    for do, peer in orient_peers:
        stat_copy(do, peer).start()

    def ag_slot(b, way, step):
        return sum(sum(h) for h in AG_HOPS[:b]) + (AG_HOPS[b][0] if way else 0) + step - 1

    def ag_copy(b, way, step):
        sign = 1 if way else -1
        c = lax.rem(z - sign * (step - 1) + NZ, NZ)
        return pltpu.make_async_remote_copy(
            src_ref=all_e.at[c, b],
            dst_ref=all_e.at[c, b],
            send_sem=ag_send,
            recv_sem=ag_recv.at[ag_slot(b, way, step)],
            device_id=at_z(sign),
            device_id_type=MESH,
        )

    def ag_step(step):
        for b in range(NB):
            for way in range(2):
                hops = AG_HOPS[b][way]
                if 1 <= step <= hops:
                    ag_copy(b, way, step).wait_recv()
                if step < hops:
                    ag_copy(b, way, step + 1).start()

    ag_step(0)
    ag_step(1)
    ag_step(2)

    pltpu.make_async_copy(stat_all, stat_all, st_recv).wait()
    big = m_row
    for j in range(NORIENT - 1):
        big = jnp.maximum(big, stat_all[j, 0:1, :])
    whole = s_row * jnp.exp(m_row - big)
    for j in range(NORIENT - 1):
        whole = whole + stat_all[j, 4:5, :] * jnp.exp(stat_all[j, 0:1, :] - big)
    lane = lax.broadcasted_iota(jnp.int32, (1, 128), 1)
    whole = jnp.where(lane < OWN, whole, 1.0)
    factor = jnp.exp(m_row - big) / whole
    fac_own[...] = jnp.broadcast_to(factor, (8, 128))

    def fac_copy(dz):
        return pltpu.make_async_remote_copy(
            src_ref=fac_own,
            dst_ref=fac_all.at[z],
            send_sem=fc_send,
            recv_sem=fc_recv,
            device_id=at_z(dz),
            device_id_type=MESH,
        )

    for dz in (4, 3, 5, 2, 6, 1, 7):
        fac_copy(dz).start()
    fac_all[z] = fac_own[...]

    ag_step(3)
    ag_step(4)
    fac_sent = fac_all.at[pl.ds(0, NZ - 1)]
    pltpu.make_async_copy(fac_sent, fac_sent, fc_recv).wait()

    cols = []
    for zz in range(NZ):
        f = jnp.sum(jnp.where(eye, fac_all[zz, 0:1, :], 0.0), axis=1, keepdims=True)
        cols.append(f)
    for b in range(NB):
        block = jnp.concatenate(
            [all_e[zz, b].astype(jnp.float32) * cols[zz] for zz in range(NZ)], axis=0
        )
        probs_ref[b * BS : (b + 1) * BS, :] = block.T.astype(jnp.bfloat16)

    pltpu.make_async_copy(recv, recv, rs_send).wait()
    pltpu.make_async_copy(y_out, y_out, y_send).wait()
    e_sent = all_e.at[pl.ds(0, NZ - 1)]
    pltpu.make_async_copy(e_sent, e_sent, ag_send).wait()
    pltpu.make_async_copy(stat_all, stat_all, st_send).wait()
    pltpu.make_async_copy(fac_sent, fac_sent, fc_send).wait()


NU = 8
UC = COLS // NU


def update_kernel(probs_ref, counts_ref, held_ref, out_ref, done, sem):
    norm = jnp.sum(probs_ref[...].astype(jnp.float32), axis=1, keepdims=True)
    inv = jnp.broadcast_to(1.0 / (norm + 1.0), (ROWS, 128))
    scale = jnp.concatenate([inv] * (UC // 128), axis=1)

    def put(u):
        return pltpu.make_async_copy(done.at[u], out_ref.at[:, pl.ds(u * UC, UC)], sem.at[u])

    for u in range(NU):
        k, c = divmod(u * UC, KC)
        num = jnp.dot(
            probs_ref[...], counts_ref[k, :, c : c + UC], preferred_element_type=jnp.float32
        )
        for b in range(NB):
            rows = slice(b * BS, (b + 1) * BS)
            x = held_ref[b, k, :, c : c + UC].astype(jnp.float32)
            done[u, rows, :] = ((num[rows] + x) * scale[rows]).astype(jnp.bfloat16)
        put(u).start()
    for u in range(NU):
        put(u).wait()


def on_device(model, patterns):
    f32, bf16 = jnp.float32, jnp.bfloat16
    dma = pltpu.SemaphoreType.DMA
    vmem = pl.BlockSpec(memory_space=pltpu.VMEM)
    hbm = pl.BlockSpec(memory_space=pltpu.HBM)
    rs_slots = sum(sum(h) for h in RS_HOPS)
    ag_slots = sum(sum(h) for h in AG_HOPS)
    probs, counts, held = pl.pallas_call(
        exchange_kernel,
        name="exchange",
        out_shape=(
            jax.ShapeDtypeStruct((ROWS, FRAMES), bf16),
            jax.ShapeDtypeStruct((NK, FRAMES, KC), bf16),
            jax.ShapeDtypeStruct((NB, NK, BS, KC), bf16),
        ),
        in_specs=[hbm] * 2,
        out_specs=(vmem,) * 3,
        scratch_shapes=[
            pltpu.VMEM((NK, FRAMES, KC), jnp.int32),
            pltpu.VMEM((NB, FRAMES, BS), f32),
            pltpu.VMEM((NB, BS, 128), f32),
            pltpu.VMEM((rs_slots, OWN, BS), f32),
            pltpu.VMEM((NB, OWN, BS), f32),
            pltpu.VMEM((NB, OWN, BS), f32),
            pltpu.VMEM((NZ, NB, OWN, BS), bf16),
            pltpu.VMEM((8, 128), f32),
            pltpu.VMEM((NORIENT - 1, 8, 128), f32),
            pltpu.VMEM((8, 128), f32),
            pltpu.VMEM((NZ, 8, 128), f32),
            dma((NK,)),
            dma((NB, NK)),
            dma,
            dma((rs_slots,)),
            dma,
            dma((NB,)),
            dma,
            dma((ag_slots,)),
            dma,
            dma,
            dma,
            dma,
        ],
        compiler_params=pltpu.CompilerParams(
            collective_id=0, has_side_effects=True, vmem_limit_bytes=40 * 1024 * 1024
        ),
    )(model, patterns)
    return pl.pallas_call(
        update_kernel,
        name="update",
        out_shape=jax.ShapeDtypeStruct((ROWS, COLS), bf16),
        in_specs=[vmem] * 3,
        out_specs=hbm,
        scratch_shapes=[pltpu.VMEM((NU, ROWS, UC), bf16), dma((NU,))],
        compiler_params=pltpu.CompilerParams(vmem_limit_bytes=30 * 1024 * 1024),
    )(probs, counts, held)


def solution(mesh):
    placed = (P("orient", "pix"), P(None, "pix"))
    return jax.shard_map(
        on_device, mesh=mesh, in_specs=placed, out_specs=P("orient", "pix"), check_vma=False
    )
```

time: 66.1 us -> 55.7 us (0.84); the launches traced: 65 us -> 55.7 us
  Pallas kernels: 62.2 us -> 55.7 us
  local copies, waits for them, and re-layouts: 2.78 us -> 0 us
    pallas_call x1, Pallas kernels: 55.3 us -> 51.3 us  [on_device(): pl.pallas_call(exchange_kernel, name='exchange', out_shape=(jax.ShapeDtyp...]
    unnamed x2 -> x0, local copies, waits for them, and re-layouts: 2.78 us -> none
    pallas_call x1, Pallas kernels: 6.91 us -> 4.39 us  [on_device(): pl.pallas_call(update_kernel, name='update', out_shape=jax.ShapeDtypeStru...]
where the time goes in v2:
time: 55.7 us
  Pallas kernels  55.7 us (100%)
    pallas_call x1, Pallas kernels, on_device(): pl.pallas_call(exchange_kernel, name='exchange', out_shape=(jax.ShapeDtyp...  51.3 us
    pallas_call x1, Pallas kernels, on_device(): pl.pallas_call(update_kernel, name='update', out_shape=jax.ShapeDtypeStru...  4.39 us

profile of v2, /device:TPU:6, one launch (start us, length us, event | category | flops | bytes accessed | tf_op | source)
XLA Modules:
  0.0 55.7 jit_solution(729562699119669594)
XLA Ops:
  0.0 51.3 %exchange.1 = (bf16[768,384]{1,0:T(8,128)(2,1)S(1)}, bf16[8,384,512]{2,1,0:T(8,128)(2,1)S(1)}, bf16[3,8,256,512]{3,2,1,0:T(8,128)(2,1)S(1)}) custom-call(bf16[768,4096]{1,0:T(8,128)(2,1)} %model_ref.1, s32[384,4096]{1,0:T(8,128)} %pat_ref.1), custom_call_target="tpu_custom_call" | custom-call | tf_op jit(solution)/shard_map/exchange/pallas_call | solution.py:372
  51.3 4.4 %update.1 = bf16[768,4096]{1,0:T(8,128)(2,1)} custom-call(bf16[768,384]{1,0:T(8,128)(2,1)S(1)} %get-tuple-element.8.probs_ref, bf16[8,384,512]{2,1,0:T(8,128)(2,1)S(1)} %get-tuple-element.9.counts_ref, bf16[3,8,256,512]{3,2,1,0:T(8,128)(2,1)S(1)} %get-tuple-element.10.held_ref), custom_call_target="tpu_custom_call" | custom-call | tf_op jit(solution)/shard_map/update/pallas_call | solution.py:411

commit v3 on v2

--- a/solution.py
+++ b/solution.py
@@ -21,7 +21,6 @@
 NZ = 8
 OWN = FRAMES // NZ
 NORIENT = 16
-UNROLL = 4
 
 RS_HOPS = ((4, 3), (3, 4), (4, 3))
 AG_HOPS = ((4, 3), (3, 4), (4, 3))
@@ -73,19 +72,14 @@
             pat_ref.at[:, pl.ds(k * KC, KC)], pv.at[k], pat_sem.at[k]
         )
 
-    def mod_copy(b, k):
+    def mod_copy(k):
         return pltpu.make_async_copy(
-            model_ref.at[pl.ds(b * BS, BS), pl.ds(k * KC, KC)],
-            mv.at[b, k],
-            mod_sem.at[b, k],
+            model_ref.at[:, pl.ds(k * KC, KC)], mv.at[k], mod_sem.at[k]
         )
 
     for k in range(NK):
         pat_copy(k).start()
-        mod_copy(0, k).start()
-    for b in range(1, NB):
-        for k in range(NK):
-            mod_copy(b, k).start()
+        mod_copy(k).start()
 
     barrier = pltpu.get_barrier_semaphore()
     for dz in range(1, NZ):
@@ -150,52 +144,42 @@
 
     ones = jnp.ones((8, 128), jnp.float32)
 
-    def chunk(b, k):
-        if b == 0:
-            mod_copy(b, k).wait()
-            pat_copy(k).wait()
-            cb[k] = pv[k].astype(jnp.float32).astype(jnp.bfloat16)
-        x = mv[b, k].astype(jnp.float32)
-        t = tot[b]
+    def chunk(k, carry):
+        mod_copy(k).wait()
+        pat_copy(k).wait()
+        c = pv[k].astype(jnp.float32).astype(jnp.bfloat16)
+        cb[k] = c
+        x = mv[k].astype(jnp.float32)
+        t = tot[...]
         for j in range(KC // 128):
             t = t + x[:, j * 128 : (j + 1) * 128]
-        tot[b] = t
+        tot[...] = t
         logs = jnp.log(x)
         hi = logs.astype(jnp.bfloat16)
         lo = (logs - hi.astype(jnp.float32)).astype(jnp.bfloat16)
-        c = cb[k]
-        part[b] += lax.dot_general(
-            jnp.concatenate([c, c], axis=1),
-            jnp.concatenate([hi, lo], axis=1),
-            (((1,), (1,)), ((), ())),
-            preferred_element_type=jnp.float32,
-        )
+        twice = jnp.concatenate([c, c], axis=1)
+        for b in range(NB):
+            rows = slice(b * BS, (b + 1) * BS)
+            part[b] += lax.dot_general(
+                twice,
+                jnp.concatenate([hi[rows], lo[rows]], axis=1),
+                (((1,), (1,)), ((), ())),
+                preferred_element_type=jnp.float32,
+            )
+        return carry
 
     def finish(b):
         row = lax.dot_general(
             ones,
-            tot[b],
+            tot[b * BS : (b + 1) * BS],
             (((1,), (1,)), ((), ())),
             precision=lax.Precision.HIGHEST,
             preferred_element_type=jnp.float32,
         )
         part[b] -= row[0:1, :]
 
-    hooks = {(1, 4): [("step", 0, 1)], (2, 4): [("step", 0, 2), ("step", 1, 1)]}
-    tail = [
-        ("step", 2, 1),
-        ("step", 1, 2),
-        ("step", 0, 3),
-        ("step", 2, 2),
-        ("step", 1, 3),
-        ("step", 0, 4),
-        ("end", 0),
-        ("step", 2, 3),
-        ("step", 1, 4),
-        ("end", 1),
-        ("step", 2, 4),
-        ("end", 2),
-    ]
+    tail = [("step", b, step) for step in range(1, 5) for b in range(NB)]
+    tail = tail[:-2] + [("end", 0)] + tail[-2:-1] + [("end", 1)] + tail[-1:] + [("end", 2)]
 
     def act(hook):
         kind, b = hook[0], hook[1]
@@ -209,18 +193,9 @@
             rs_end(b)
 
     tot[...] = jnp.zeros_like(tot)
+    part[...] = jnp.zeros_like(part)
+    lax.fori_loop(0, NK, chunk, 0)
     for b in range(NB):
-        part[b] = jnp.zeros((FRAMES, BS), jnp.float32)
-        if b == 0:
-            lax.fori_loop(0, NK, lambda k, carry: (chunk(0, k), carry)[1], 0)
-        else:
-            for k in range(NK):
-                mod_copy(b, k).wait()
-            for first in range(0, NK, UNROLL):
-                for k in range(first, first + UNROLL):
-                    chunk(b, k)
-                for hook in hooks.get((b, first), ()):
-                    act(hook)
         finish(b)
         act(("start", b))
     for hook in tail:
@@ -355,7 +330,7 @@
         )
         for b in range(NB):
             rows = slice(b * BS, (b + 1) * BS)
-            x = held_ref[b, k, :, c : c + UC].astype(jnp.float32)
+            x = held_ref[k, rows, c : c + UC].astype(jnp.float32)
             done[u, rows, :] = ((num[rows] + x) * scale[rows]).astype(jnp.bfloat16)
         put(u).start()
     for u in range(NU):
@@ -375,14 +350,14 @@
         out_shape=(
             jax.ShapeDtypeStruct((ROWS, FRAMES), bf16),
             jax.ShapeDtypeStruct((NK, FRAMES, KC), bf16),
-            jax.ShapeDtypeStruct((NB, NK, BS, KC), bf16),
+            jax.ShapeDtypeStruct((NK, ROWS, KC), bf16),
         ),
         in_specs=[hbm] * 2,
         out_specs=(vmem,) * 3,
         scratch_shapes=[
             pltpu.VMEM((NK, FRAMES, KC), jnp.int32),
             pltpu.VMEM((NB, FRAMES, BS), f32),
-            pltpu.VMEM((NB, BS, 128), f32),
+            pltpu.VMEM((ROWS, 128), f32),
             pltpu.VMEM((rs_slots, OWN, BS), f32),
             pltpu.VMEM((NB, OWN, BS), f32),
             pltpu.VMEM((NB, OWN, BS), f32),
@@ -392,7 +367,7 @@
             pltpu.VMEM((8, 128), f32),
             pltpu.VMEM((NZ, 8, 128), f32),
             dma((NK,)),
-            dma((NB, NK)),
+            dma((NK,)),
             dma,
             dma((rs_slots,)),
             dma,

time: 55.7 us -> 52.3 us (0.939)
  Pallas kernels: 55.7 us -> 52.1 us
    pallas_call x1, Pallas kernels: 51.3 us -> 47.7 us  [on_device(): pl.pallas_call(exchange_kernel, name='exchange', out_shape=(jax.ShapeDtyp...]
where the time goes in v3:
time: 52.3 us; the launch traced here: 52.1 us
  Pallas kernels  52.1 us (100%)
    pallas_call x1, Pallas kernels, on_device(): pl.pallas_call(exchange_kernel, name='exchange', out_shape=(jax.ShapeDtyp...  47.7 us
    pallas_call x1, Pallas kernels, on_device(): pl.pallas_call(update_kernel, name='update', out_shape=jax.ShapeDtypeStru...  4.39 us

profile of v3, /device:TPU:6, one launch (start us, length us, event | category | flops | bytes accessed | tf_op | source)
XLA Modules:
  0.0 52.1 jit_solution(7517710237497123541)
XLA Ops:
  0.0 47.7 %exchange.1 = (bf16[768,384]{1,0:T(8,128)(2,1)S(1)}, bf16[8,384,512]{2,1,0:T(8,128)(2,1)S(1)}, bf16[8,768,512]{2,1,0:T(8,128)(2,1)S(1)}) custom-call(bf16[768,4096]{1,0:T(8,128)(2,1)} %model_ref.1, s32[384,4096]{1,0:T(8,128)} %pat_ref.1), custom_call_target="tpu_custom_call" | custom-call | tf_op jit(solution)/shard_map/exchange/pallas_call | solution.py:347
  47.7 4.4 %update.1 = bf16[768,4096]{1,0:T(8,128)(2,1)} custom-call(bf16[768,384]{1,0:T(8,128)(2,1)S(1)} %get-tuple-element.8.probs_ref, bf16[8,384,512]{2,1,0:T(8,128)(2,1)S(1)} %get-tuple-element.9.counts_ref, bf16[8,768,512]{2,1,0:T(8,128)(2,1)S(1)} %get-tuple-element.10.held_ref), custom_call_target="tpu_custom_call" | custom-call | tf_op jit(solution)/shard_map/update/pallas_call | solution.py:386

commit v4 on v3

--- a/solution.py
+++ b/solution.py
@@ -23,7 +23,6 @@
 NORIENT = 16
 
 RS_HOPS = ((4, 3), (3, 4), (4, 3))
-AG_HOPS = ((4, 3), (3, 4), (4, 3))
 
 
 def exchange_kernel(
@@ -43,6 +42,7 @@
     stat_all,
     fac_own,
     fac_all,
+    turned,
     pat_sem,
     mod_sem,
     rs_send,
@@ -168,15 +168,17 @@
             )
         return carry
 
-    def finish(b):
+    def finish():
         row = lax.dot_general(
             ones,
-            tot[b * BS : (b + 1) * BS],
+            tot[...],
             (((1,), (1,)), ((), ())),
             precision=lax.Precision.HIGHEST,
             preferred_element_type=jnp.float32,
         )
-        part[b] -= row[0:1, :]
+        for b in range(NB):
+            part[b] -= row[0:1, b * BS : (b + 1) * BS]
+            act(("start", b))
 
     tail = [("step", b, step) for step in range(1, 5) for b in range(NB)]
     tail = tail[:-2] + [("end", 0)] + tail[-2:-1] + [("end", 1)] + tail[-1:] + [("end", 2)]
@@ -195,17 +197,24 @@
     tot[...] = jnp.zeros_like(tot)
     part[...] = jnp.zeros_like(part)
     lax.fori_loop(0, NK, chunk, 0)
-    for b in range(NB):
-        finish(b)
-        act(("start", b))
+    finish()
     for hook in tail:
         act(hook)
 
+    def ag_copy(b, dz):
+        return pltpu.make_async_remote_copy(
+            src_ref=all_e.at[z, b],
+            dst_ref=all_e.at[z, b],
+            send_sem=ag_send,
+            recv_sem=ag_recv,
+            device_id=at_z(dz),
+            device_id_type=MESH,
+        )
+
     scores = []
     for b in range(NB):
         y_copy(b).wait_recv()
         scores.append(BETA * (y_out[b] + y_in[b]))
-
     m = jnp.max(jnp.maximum(jnp.maximum(scores[0], scores[1]), scores[2]), axis=1, keepdims=True)
     acc = jnp.zeros((OWN, BS), jnp.float32)
     for b in range(NB):
@@ -213,13 +222,11 @@
         acc = acc + e
         all_e[z, b] = e.astype(jnp.bfloat16)
     esum = jnp.sum(acc, axis=1, keepdims=True)
-    eye = lax.broadcasted_iota(jnp.int32, (OWN, 128), 0) == lax.broadcasted_iota(
-        jnp.int32, (OWN, 128), 1
+    row = lax.broadcasted_iota(jnp.int32, (OWN, 128), 0)
+    lane = lax.broadcasted_iota(jnp.int32, (OWN, 128), 1)
+    stat_own[...] = jnp.sum(
+        jnp.where(lane == row, m, jnp.where(lane == row + 64, esum, 0.0)), axis=0, keepdims=True
     )
-    m_row = jnp.sum(jnp.where(eye, m, 0.0), axis=0, keepdims=True)
-    s_row = jnp.sum(jnp.where(eye, esum, 0.0), axis=0, keepdims=True)
-    upper = lax.broadcasted_iota(jnp.int32, (8, 128), 0) < 4
-    stat_own[...] = jnp.where(upper, m_row, s_row)
 
     def stat_copy(do, peer):
         return pltpu.make_async_remote_copy(
@@ -233,46 +240,19 @@
 
     for do, peer in orient_peers:
         stat_copy(do, peer).start()
-
-    def ag_slot(b, way, step):
-        return sum(sum(h) for h in AG_HOPS[:b]) + (AG_HOPS[b][0] if way else 0) + step - 1
-
-    def ag_copy(b, way, step):
-        sign = 1 if way else -1
-        c = lax.rem(z - sign * (step - 1) + NZ, NZ)
-        return pltpu.make_async_remote_copy(
-            src_ref=all_e.at[c, b],
-            dst_ref=all_e.at[c, b],
-            send_sem=ag_send,
-            recv_sem=ag_recv.at[ag_slot(b, way, step)],
-            device_id=at_z(sign),
-            device_id_type=MESH,
-        )
-
-    def ag_step(step):
-        for b in range(NB):
-            for way in range(2):
-                hops = AG_HOPS[b][way]
-                if 1 <= step <= hops:
-                    ag_copy(b, way, step).wait_recv()
-                if step < hops:
-                    ag_copy(b, way, step + 1).start()
-
-    ag_step(0)
-    ag_step(1)
-    ag_step(2)
-
-    pltpu.make_async_copy(stat_all, stat_all, st_recv).wait()
-    big = m_row
-    for j in range(NORIENT - 1):
-        big = jnp.maximum(big, stat_all[j, 0:1, :])
-    whole = s_row * jnp.exp(m_row - big)
-    for j in range(NORIENT - 1):
-        whole = whole + stat_all[j, 4:5, :] * jnp.exp(stat_all[j, 0:1, :] - big)
-    lane = lax.broadcasted_iota(jnp.int32, (1, 128), 1)
-    whole = jnp.where(lane < OWN, whole, 1.0)
-    factor = jnp.exp(m_row - big) / whole
-    fac_own[...] = jnp.broadcast_to(factor, (8, 128))
+    for b in range(NB):
+        for dz in (4, 3, 5, 2, 6, 1, 7):
+            ag_copy(b, dz).start()
+
+    stat_all[NORIENT - 1] = stat_own[...]
+    stats_sent = stat_all.at[pl.ds(0, NORIENT - 1)]
+    pltpu.make_async_copy(stats_sent, stats_sent, st_recv).wait()
+    stats = stat_all[:, 0, :]
+    big = jnp.max(stats, axis=0, keepdims=True)
+    weight = jnp.exp(stats - big)
+    whole = jnp.sum(pltpu.roll(stats, 64, 1) * weight, axis=0, keepdims=True)
+    used = lax.broadcasted_iota(jnp.int32, (1, 128), 1) < OWN
+    fac_own[...] = jnp.where(used, jnp.exp(stat_own[...] - big) / jnp.where(used, whole, 1.0), 0.0)
 
     def fac_copy(dz):
         return pltpu.make_async_remote_copy(
@@ -288,26 +268,27 @@
         fac_copy(dz).start()
     fac_all[z] = fac_own[...]
 
-    ag_step(3)
-    ag_step(4)
+    e_sent = all_e.at[pl.ds(0, NZ - 1)]
     fac_sent = fac_all.at[pl.ds(0, NZ - 1)]
+    pltpu.make_async_copy(e_sent, e_sent, ag_recv).wait()
+    for b in range(NB):
+        block = jnp.concatenate([all_e[zz, b].astype(jnp.float32) for zz in range(NZ)], axis=0)
+        turned[b * BS : (b + 1) * BS, :] = block.T
+
     pltpu.make_async_copy(fac_sent, fac_sent, fc_recv).wait()
-
-    cols = []
+    pad = jnp.zeros((1, FRAMES - 128), jnp.float32)
+    factors = jnp.zeros((1, FRAMES), jnp.float32)
     for zz in range(NZ):
-        f = jnp.sum(jnp.where(eye, fac_all[zz, 0:1, :], 0.0), axis=1, keepdims=True)
-        cols.append(f)
-    for b in range(NB):
-        block = jnp.concatenate(
-            [all_e[zz, b].astype(jnp.float32) * cols[zz] for zz in range(NZ)], axis=0
-        )
-        probs_ref[b * BS : (b + 1) * BS, :] = block.T.astype(jnp.bfloat16)
+        piece = jnp.concatenate([fac_all[zz], pad], axis=1)
+        factors = factors + (pltpu.roll(piece, zz * OWN, 1) if zz else piece)
+    for b in range(NB):
+        rows = slice(b * BS, (b + 1) * BS)
+        probs_ref[rows, :] = (turned[rows, :] * factors).astype(jnp.bfloat16)
 
     pltpu.make_async_copy(recv, recv, rs_send).wait()
     pltpu.make_async_copy(y_out, y_out, y_send).wait()
-    e_sent = all_e.at[pl.ds(0, NZ - 1)]
     pltpu.make_async_copy(e_sent, e_sent, ag_send).wait()
-    pltpu.make_async_copy(stat_all, stat_all, st_send).wait()
+    pltpu.make_async_copy(stats_sent, stats_sent, st_send).wait()
     pltpu.make_async_copy(fac_sent, fac_sent, fc_send).wait()
 
 
@@ -343,7 +324,6 @@
     vmem = pl.BlockSpec(memory_space=pltpu.VMEM)
     hbm = pl.BlockSpec(memory_space=pltpu.HBM)
     rs_slots = sum(sum(h) for h in RS_HOPS)
-    ag_slots = sum(sum(h) for h in AG_HOPS)
     probs, counts, held = pl.pallas_call(
         exchange_kernel,
         name="exchange",
@@ -362,10 +342,11 @@
             pltpu.VMEM((NB, OWN, BS), f32),
             pltpu.VMEM((NB, OWN, BS), f32),
             pltpu.VMEM((NZ, NB, OWN, BS), bf16),
-            pltpu.VMEM((8, 128), f32),
-            pltpu.VMEM((NORIENT - 1, 8, 128), f32),
-            pltpu.VMEM((8, 128), f32),
-            pltpu.VMEM((NZ, 8, 128), f32),
+            pltpu.VMEM((1, 128), f32),
+            pltpu.VMEM((NORIENT, 1, 128), f32),
+            pltpu.VMEM((1, 128), f32),
+            pltpu.VMEM((NZ, 1, 128), f32),
+            pltpu.VMEM((ROWS, FRAMES), f32),
             dma((NK,)),
             dma((NK,)),
             dma,
@@ -373,7 +354,7 @@
             dma,
             dma((NB,)),
             dma,
-            dma((ag_slots,)),
+            dma,
             dma,
             dma,
             dma,

time: 52.3 us -> 51 us (0.975); the launches traced: 52.1 us -> 50 us
  Pallas kernels: 52.1 us -> 50 us
    pallas_call x1, Pallas kernels: 47.7 us -> 45.6 us  [on_device(): pl.pallas_call(exchange_kernel, name='exchange', out_shape=(jax.ShapeDtyp...]
where the time goes in v4:
time: 51 us; the launch traced here: 50 us
  Pallas kernels  50 us (98%)
    pallas_call x1, Pallas kernels, on_device(): pl.pallas_call(exchange_kernel, name='exchange', out_shape=(jax.ShapeDtyp...  45.6 us
    pallas_call x1, Pallas kernels, on_device(): pl.pallas_call(update_kernel, name='update', out_shape=jax.ShapeDtypeStru...  4.39 us

profile of v4, /device:TPU:6, one launch (start us, length us, event | category | flops | bytes accessed | tf_op | source)
XLA Modules:
  0.0 50.0 jit_solution(11226680169001469357)
XLA Ops:
  0.0 45.6 %exchange.1 = (bf16[768,384]{1,0:T(8,128)(2,1)S(1)}, bf16[8,384,512]{2,1,0:T(8,128)(2,1)S(1)}, bf16[8,768,512]{2,1,0:T(8,128)(2,1)S(1)}) custom-call(bf16[768,4096]{1,0:T(8,128)(2,1)} %model_ref.1, s32[384,4096]{1,0:T(8,128)} %pat_ref.1), custom_call_target="tpu_custom_call" | custom-call | tf_op jit(solution)/shard_map/exchange/pallas_call | solution.py:327
  45.6 4.4 %update.1 = bf16[768,4096]{1,0:T(8,128)(2,1)} custom-call(bf16[768,384]{1,0:T(8,128)(2,1)S(1)} %get-tuple-element.8.probs_ref, bf16[8,384,512]{2,1,0:T(8,128)(2,1)S(1)} %get-tuple-element.9.counts_ref, bf16[8,768,512]{2,1,0:T(8,128)(2,1)S(1)} %get-tuple-element.10.held_ref), custom_call_target="tpu_custom_call" | custom-call | tf_op jit(solution)/shard_map/update/pallas_call | solution.py:367

commit v5 on v4

--- a/solution.py
+++ b/solution.py
@@ -22,7 +22,7 @@
 OWN = FRAMES // NZ
 NORIENT = 16
 
-RS_HOPS = ((4, 3), (3, 4), (4, 3))
+RS_HOPS = (((4, 3), (3, 4)) * 3)[:3]
 
 
 def exchange_kernel(
@@ -158,14 +158,14 @@
         hi = logs.astype(jnp.bfloat16)
         lo = (logs - hi.astype(jnp.float32)).astype(jnp.bfloat16)
         twice = jnp.concatenate([c, c], axis=1)
+        d = lax.dot_general(
+            twice,
+            jnp.concatenate([hi, lo], axis=1),
+            (((1,), (1,)), ((), ())),
+            preferred_element_type=jnp.float32,
+        )
         for b in range(NB):
-            rows = slice(b * BS, (b + 1) * BS)
-            part[b] += lax.dot_general(
-                twice,
-                jnp.concatenate([hi[rows], lo[rows]], axis=1),
-                (((1,), (1,)), ((), ())),
-                preferred_element_type=jnp.float32,
-            )
+            part[b] += d[:, b * BS : (b + 1) * BS]
         return carry
 
     def finish():
@@ -180,8 +180,9 @@
             part[b] -= row[0:1, b * BS : (b + 1) * BS]
             act(("start", b))
 
-    tail = [("step", b, step) for step in range(1, 5) for b in range(NB)]
-    tail = tail[:-2] + [("end", 0)] + tail[-2:-1] + [("end", 1)] + tail[-1:] + [("end", 2)]
+    tail = [("step", b, step) for step in range(1, 4) for b in range(NB)]
+    for b in range(NB):
+        tail += [("step", b, 4), ("end", b)]
 
     def act(hook):
         kind, b = hook[0], hook[1]
@@ -215,7 +216,10 @@
     for b in range(NB):
         y_copy(b).wait_recv()
         scores.append(BETA * (y_out[b] + y_in[b]))
-    m = jnp.max(jnp.maximum(jnp.maximum(scores[0], scores[1]), scores[2]), axis=1, keepdims=True)
+    top = scores[0]
+    for b in range(1, NB):
+        top = jnp.maximum(top, scores[b])
+    m = jnp.max(top, axis=1, keepdims=True)
     acc = jnp.zeros((OWN, BS), jnp.float32)
     for b in range(NB):
         e = jnp.exp(scores[b] - m)

time: 51 us -> 50.4 us (0.988); the launches traced: 50 us -> 50 us
  no operation moved by 1% of the time
where the time goes in v5:
time: 50.4 us; the launch traced here: 50 us
  Pallas kernels  50 us (99%)
    pallas_call x1, Pallas kernels, on_device(): pl.pallas_call(exchange_kernel, name='exchange', out_shape=(jax.ShapeDtyp...  45.6 us
    pallas_call x1, Pallas kernels, on_device(): pl.pallas_call(update_kernel, name='update', out_shape=jax.ShapeDtypeStru...  4.39 us

profile of v5, /device:TPU:6, one launch (start us, length us, event | category | flops | bytes accessed | tf_op | source)
XLA Modules:
  0.0 50.0 jit_solution(8989348530335260535)
XLA Ops:
  0.0 45.6 %exchange.1 = (bf16[768,384]{1,0:T(8,128)(2,1)S(1)}, bf16[8,384,512]{2,1,0:T(8,128)(2,1)S(1)}, bf16[8,768,512]{2,1,0:T(8,128)(2,1)S(1)}) custom-call(bf16[768,4096]{1,0:T(8,128)(2,1)} %model_ref.1, s32[384,4096]{1,0:T(8,128)} %pat_ref.1), custom_call_target="tpu_custom_call" | custom-call | tf_op jit(solution)/shard_map/exchange/pallas_call | solution.py:331
  45.6 4.4 %update.1 = bf16[768,4096]{1,0:T(8,128)(2,1)} custom-call(bf16[768,384]{1,0:T(8,128)(2,1)S(1)} %get-tuple-element.8.probs_ref, bf16[8,384,512]{2,1,0:T(8,128)(2,1)S(1)} %get-tuple-element.9.counts_ref, bf16[8,768,512]{2,1,0:T(8,128)(2,1)S(1)} %get-tuple-element.10.held_ref), custom_call_target="tpu_custom_call" | custom-call | tf_op jit(solution)/shard_map/update/pallas_call | solution.py:371

commit v6 on v5

--- a/solution.py
+++ b/solution.py
@@ -65,7 +65,8 @@
         return (o, y * NZ + lax.rem(z + dz + NZ, NZ))
 
     y_peer = (o, (1 - y) * NZ + z)
-    orient_peers = [(do, (lax.rem(o + do, NORIENT), p)) for do in range(1, NORIENT)]
+    far_first = (11, 10, 9, 8, 7, 6, 5, 14, 15, 13, 12, 4, 3, 2, 1)
+    orient_peers = [(do, (lax.rem(o + do, NORIENT), p)) for do in far_first]
 
     def pat_copy(k):
         return pltpu.make_async_copy(

time: 50.4 us -> 50.4 us (level)
  no operation moved by 1% of the time
where the time goes in v6:
time: 50.4 us; the launch traced here: 50 us
  Pallas kernels  50 us (99%)
    pallas_call x1, Pallas kernels, on_device(): pl.pallas_call(exchange_kernel, name='exchange', out_shape=(jax.ShapeDtyp...  45.6 us
    pallas_call x1, Pallas kernels, on_device(): pl.pallas_call(update_kernel, name='update', out_shape=jax.ShapeDtypeStru...  4.39 us

profile of v6, /device:TPU:6, one launch (start us, length us, event | category | flops | bytes accessed | tf_op | source)
XLA Modules:
  0.0 50.0 jit_solution(12782859047524827318)
XLA Ops:
  0.0 45.6 %exchange.1 = (bf16[768,384]{1,0:T(8,128)(2,1)S(1)}, bf16[8,384,512]{2,1,0:T(8,128)(2,1)S(1)}, bf16[8,768,512]{2,1,0:T(8,128)(2,1)S(1)}) custom-call(bf16[768,4096]{1,0:T(8,128)(2,1)} %model_ref.1, s32[384,4096]{1,0:T(8,128)} %pat_ref.1), custom_call_target="tpu_custom_call" | custom-call | tf_op jit(solution)/shard_map/exchange/pallas_call | solution.py:332
  45.6 4.4 %update.1 = bf16[768,4096]{1,0:T(8,128)(2,1)} custom-call(bf16[768,384]{1,0:T(8,128)(2,1)S(1)} %get-tuple-element.8.probs_ref, bf16[8,384,512]{2,1,0:T(8,128)(2,1)S(1)} %get-tuple-element.9.counts_ref, bf16[8,768,512]{2,1,0:T(8,128)(2,1)S(1)} %get-tuple-element.10.held_ref), custom_call_target="tpu_custom_call" | custom-call | tf_op jit(solution)/shard_map/update/pallas_call | solution.py:372
